TPU v7x, 32 devices: a whole 2x2x4 slice. The times are simulated.
32 devices in a mesh: dp: 16 (over z, x, core), seq: 2 (over y).
Axes of the slice: x: 2, y: 2, z: 4, core: 2. Of those that a mesh axis runs over, the one named last changes fastest.
Arguments:
- frames_in: bfloat16 [16, 1500, 768], P('dp', 'seq'), may hold values from -6 to 6
- ln1_gain: bfloat16 [768], P('dp'), may hold values from 0.25 to 1.75
- ln1_bias: bfloat16 [768], P('dp'), may hold values from -1.75 to 1.75
- w_qkv: bfloat16 [768, 2304], P('dp'), may hold values from -2 to 2
- b_qv: bfloat16 [1536], P('dp'), may hold values from -1.25 to 1.25
- w_o: bfloat16 [768, 768], P('dp'), may hold values from -0.875 to 0.875
- b_o: bfloat16 [768], P('dp'), may hold values from -1.75 to 1.75
- ln2_gain: bfloat16 [768], P('dp'), may hold values from 0.25 to 1.75
- ln2_bias: bfloat16 [768], P('dp'), may hold values from -1.75 to 1.75
- w_fc1: bfloat16 [768, 3072], P('dp'), may hold values from -0.21875 to 0.21875
- b_fc1: bfloat16 [3072], P('dp'), may hold values from -3 to 3
- w_fc2: bfloat16 [3072, 768], P('dp'), may hold values from -0.109375 to 0.109375
- b_fc2: bfloat16 [768], P('dp'), may hold values from -1.75 to 1.75
- cotangent: bfloat16 [16, 1500, 768], P('dp', 'seq'), may hold values from -6 to 6
Outputs:
- frames_out: bfloat16 [16, 1500, 768], P('dp', 'seq')
- grad_frames: float32 [16, 1500, 768], P('dp', 'seq')
- grad_ln1_gain: float32 [768], P('dp')
- grad_ln1_bias: float32 [768], P('dp')
- grad_w_qkv: float32 [768, 2304], P('dp')
- grad_b_qv: float32 [1536], P('dp')
- grad_w_o: float32 [768, 768], P('dp')
- grad_b_o: float32 [768], P('dp')
- grad_ln2_gain: float32 [768], P('dp')
- grad_ln2_bias: float32 [768], P('dp')
- grad_w_fc1: float32 [768, 3072], P('dp')
- grad_b_fc1: float32 [3072], P('dp')
- grad_w_fc2: float32 [3072, 768], P('dp')
- grad_b_fc2: float32 [768], P('dp')
All inputs are finite; a program needn't handle non-finite values.
Results may differ from a plain program's by a relative error of at most 0.0095.
Values may be sent and summed in bfloat16 or wider, within the bound.
No kernel may reach another device: no remote copies, remote signals or barrier semaphores. Data moves between devices by JAX's collectives and lax.ppermute only.
A program may use at most 192 MiB of HBM per device.

v0:
```python
import math
import jax
import jax.numpy as jnp
from jax import lax
from jax.sharding import PartitionSpec as P

HEADS = 12
EPSILON = 1e-05


def normalize(values, gain, shift):
    center = jnp.mean(values, axis=-1, keepdims=True)
    centered = values - center
    variance = jnp.mean(centered * centered, axis=-1, keepdims=True)
    inverse = lax.rsqrt(variance + EPSILON)
    normed = centered * inverse
    return (normed, inverse, normed * gain + shift)


def norm_back(grad_out, normed, inverse, gain):
    weighted = grad_out * gain
    first = jnp.mean(weighted, axis=-1, keepdims=True)
    second = jnp.mean(weighted * normed, axis=-1, keepdims=True)
    return inverse * (weighted - first - normed * second)


def gelu_cdf(values):
    return 0.5 * (1.0 + lax.erf(values * (1.0 / math.sqrt(2.0))))


def gelu_slope(values):
    density = jnp.exp(-0.5 * values * values) * (1.0 / math.sqrt(2.0 * math.pi))
    return gelu_cdf(values) + values * density


def head_forward(operands):
    query, key_rows, value_rows = operands
    factor = 1.0 / math.sqrt(query.shape[-1])
    scores = jnp.dot(query, key_rows.T, preferred_element_type=jnp.float32) * factor
    row_peak = jnp.max(scores, axis=-1, keepdims=True)
    row_total = jnp.sum(jnp.exp(scores - row_peak), axis=-1, keepdims=True)
    logsum = row_peak + jnp.log(row_total)
    weights_low = jnp.exp(scores - logsum).astype(jnp.bfloat16)
    context = jnp.dot(weights_low, value_rows, preferred_element_type=jnp.float32).astype(
        jnp.bfloat16
    )
    return (context, logsum[:, 0])


def head_backward(operands):
    query, key_rows, value_rows, context, grad_context, logsum = operands
    factor = 1.0 / math.sqrt(query.shape[-1])
    scores = jnp.dot(query, key_rows.T, preferred_element_type=jnp.float32) * factor
    weights_full = jnp.exp(scores - logsum[:, None])
    weights_low = weights_full.astype(jnp.bfloat16)
    grad_values = jnp.dot(weights_low.T, grad_context, preferred_element_type=jnp.float32).astype(
        jnp.bfloat16
    )
    grad_weights = jnp.dot(grad_context, value_rows.T, preferred_element_type=jnp.float32)
    delta = jnp.sum(
        grad_context.astype(jnp.float32) * context.astype(jnp.float32), axis=-1, keepdims=True
    )
    grad_scores = (weights_full * (grad_weights - delta)).astype(jnp.bfloat16)
    grad_query = (
        jnp.dot(grad_scores, key_rows, preferred_element_type=jnp.float32) * factor
    ).astype(jnp.bfloat16)
    grad_keys = (jnp.dot(grad_scores.T, query, preferred_element_type=jnp.float32) * factor).astype(
        jnp.bfloat16
    )
    return (grad_query, grad_keys, grad_values)


def to_heads(block, head_size):
    clip_count, frame_count, group_width = block.shape
    split = block.reshape(clip_count, frame_count, group_width // head_size, head_size)
    return split.transpose(0, 2, 1, 3).reshape(
        clip_count * (group_width // head_size), frame_count, head_size
    )


def from_heads(block, clip_count):
    stacked, frame_count, head_size = block.shape
    group_heads = stacked // clip_count
    joined = block.reshape(clip_count, group_heads, frame_count, head_size).transpose(0, 2, 1, 3)
    return joined.reshape(clip_count, frame_count, group_heads * head_size)


def shards(
    frames_in,
    ln1_gain,
    ln1_bias,
    w_qkv,
    b_qv,
    w_o,
    b_o,
    ln2_gain,
    ln2_bias,
    w_fc1,
    b_fc1,
    w_fc2,
    b_fc2,
    cotangent,
):
    clip_count, local_frames, features = frames_in.shape
    head_size = features // HEADS
    token_rows = clip_count * local_frames
    shape_local = (clip_count, local_frames, features)
    attn_full = (
        lax.all_gather(w_qkv, "dp", axis=0, tiled=True),
        lax.all_gather(w_o, "dp", axis=0, tiled=True),
        lax.all_gather(ln1_gain, "dp", axis=0, tiled=True),
        lax.all_gather(ln1_bias, "dp", axis=0, tiled=True),
        lax.all_gather(b_qv, "dp", axis=0, tiled=True),
        lax.all_gather(b_o, "dp", axis=0, tiled=True),
    )
    qkv_full, out_full, gain_low_one, shift_low_one, bias_qv_low, bias_out_low = attn_full
    gain_one = gain_low_one.astype(jnp.float32)
    shift_one = shift_low_one.astype(jnp.float32)
    bias_wide = bias_qv_low.astype(jnp.float32)
    bias_out = bias_out_low.astype(jnp.float32)
    inputs = frames_in.reshape(token_rows, features).astype(jnp.float32)
    normed_one, inverse_one, hidden_one = normalize(inputs, gain_one, shift_one)
    hidden_one = hidden_one.astype(jnp.bfloat16)
    projected = jnp.dot(hidden_one, qkv_full, preferred_element_type=jnp.float32)
    query = (projected[:, :features] + bias_wide[:features]).astype(jnp.bfloat16)
    key_rows = projected[:, features : 2 * features].astype(jnp.bfloat16)
    value_rows = (projected[:, 2 * features :] + bias_wide[features:]).astype(jnp.bfloat16)
    query_group, key_group, value_group = (
        lax.all_to_all(query.reshape(shape_local), "seq", split_axis=2, concat_axis=1, tiled=True),
        lax.all_to_all(
            key_rows.reshape(shape_local), "seq", split_axis=2, concat_axis=1, tiled=True
        ),
        lax.all_to_all(
            value_rows.reshape(shape_local), "seq", split_axis=2, concat_axis=1, tiled=True
        ),
    )
    query_heads = to_heads(query_group, head_size)
    key_heads = to_heads(key_group, head_size)
    value_heads = to_heads(value_group, head_size)
    context_heads, logsum = lax.map(head_forward, (query_heads, key_heads, value_heads))
    context_heads = lax.optimization_barrier(context_heads)
    context = lax.all_to_all(
        from_heads(context_heads, clip_count), "seq", split_axis=1, concat_axis=2, tiled=True
    )
    context = context.reshape(token_rows, features)
    residual = inputs + jnp.dot(context, out_full, preferred_element_type=jnp.float32) + bias_out
    mlp_full = (
        lax.all_gather(w_fc1, "dp", axis=0, tiled=True),
        lax.all_gather(w_fc2, "dp", axis=0, tiled=True),
        lax.all_gather(ln2_gain, "dp", axis=0, tiled=True),
        lax.all_gather(ln2_bias, "dp", axis=0, tiled=True),
        lax.all_gather(b_fc1, "dp", axis=0, tiled=True),
        lax.all_gather(b_fc2, "dp", axis=0, tiled=True),
    )
    fc1_full, fc2_full, gain_low_two, shift_low_two, bias_fc1_low, bias_fc2_low = mlp_full
    gain_two = gain_low_two.astype(jnp.float32)
    shift_two = shift_low_two.astype(jnp.float32)
    normed_two, inverse_two, hidden_two = normalize(residual, gain_two, shift_two)
    hidden_two = hidden_two.astype(jnp.bfloat16)
    pre_act = jnp.dot(
        hidden_two, fc1_full, preferred_element_type=jnp.float32
    ) + bias_fc1_low.astype(jnp.float32)
    activated = (pre_act * gelu_cdf(pre_act)).astype(jnp.bfloat16)
    output = (
        residual
        + jnp.dot(activated, fc2_full, preferred_element_type=jnp.float32)
        + bias_fc2_low.astype(jnp.float32)
    )
    frames_out = output.astype(jnp.bfloat16).reshape(shape_local)
    grad_low = cotangent.reshape(token_rows, features)
    grad_full = grad_low.astype(jnp.float32)
    grad_bias_fc2 = jnp.sum(grad_full, axis=0)
    grad_weight_fc2 = jnp.dot(activated.T, grad_low, preferred_element_type=jnp.float32)
    grad_pre = jnp.dot(grad_low, fc2_full.T, preferred_element_type=jnp.float32) * gelu_slope(
        pre_act
    )
    grad_bias_fc1 = jnp.sum(grad_pre, axis=0)
    grad_pre_low = grad_pre.astype(jnp.bfloat16)
    grad_weight_fc1 = jnp.dot(hidden_two.T, grad_pre_low, preferred_element_type=jnp.float32)
    grad_hidden_two = jnp.dot(grad_pre_low, fc1_full.T, preferred_element_type=jnp.float32)
    grad_gain_two = jnp.sum(grad_hidden_two * normed_two, axis=0)
    grad_shift_two = jnp.sum(grad_hidden_two, axis=0)
    grad_residual = grad_full + norm_back(grad_hidden_two, normed_two, inverse_two, gain_two)
    mlp_terms = (
        grad_weight_fc1,
        grad_weight_fc2,
        grad_gain_two,
        grad_shift_two,
        grad_bias_fc1,
        grad_bias_fc2,
    )
    mlp_summed = lax.psum(
        (mlp_terms[0], mlp_terms[1], mlp_terms[2], mlp_terms[3], mlp_terms[4], mlp_terms[5]), "seq"
    )
    mlp_grads = (
        lax.psum_scatter(mlp_summed[0], "dp", scatter_dimension=0, tiled=True),
        lax.psum_scatter(mlp_summed[1], "dp", scatter_dimension=0, tiled=True),
        lax.psum_scatter(mlp_summed[2], "dp", scatter_dimension=0, tiled=True),
        lax.psum_scatter(mlp_summed[3], "dp", scatter_dimension=0, tiled=True),
        lax.psum_scatter(mlp_summed[4], "dp", scatter_dimension=0, tiled=True),
        lax.psum_scatter(mlp_summed[5], "dp", scatter_dimension=0, tiled=True),
    )
    grad_bias_out = jnp.sum(grad_residual, axis=0)
    grad_residual_low = grad_residual.astype(jnp.bfloat16)
    grad_weight_out = jnp.dot(context.T, grad_residual_low, preferred_element_type=jnp.float32)
    grad_context = jnp.dot(
        grad_residual_low, out_full.T, preferred_element_type=jnp.float32
    ).astype(jnp.bfloat16)
    grad_context_group = lax.all_to_all(
        grad_context.reshape(shape_local), "seq", split_axis=2, concat_axis=1, tiled=True
    )
    back_heads = lax.map(
        head_backward,
        (
            query_heads,
            key_heads,
            value_heads,
            context_heads,
            to_heads(grad_context_group, head_size),
            logsum,
        ),
    )
    grad_query_back, grad_keys_back, grad_values_back = (
        lax.all_to_all(
            from_heads(back_heads[0], clip_count), "seq", split_axis=1, concat_axis=2, tiled=True
        ),
        lax.all_to_all(
            from_heads(back_heads[1], clip_count), "seq", split_axis=1, concat_axis=2, tiled=True
        ),
        lax.all_to_all(
            from_heads(back_heads[2], clip_count), "seq", split_axis=1, concat_axis=2, tiled=True
        ),
    )
    grad_query = grad_query_back.reshape(token_rows, features)
    grad_keys = grad_keys_back.reshape(token_rows, features)
    grad_values = grad_values_back.reshape(token_rows, features)
    grad_bias_qv = jnp.concatenate(
        [
            jnp.sum(grad_query.astype(jnp.float32), axis=0),
            jnp.sum(grad_values.astype(jnp.float32), axis=0),
        ]
    )
    grad_projected = jnp.concatenate([grad_query, grad_keys, grad_values], axis=1)
    grad_weight_qkv = jnp.dot(hidden_one.T, grad_projected, preferred_element_type=jnp.float32)
    grad_hidden_one = jnp.dot(grad_projected, qkv_full.T, preferred_element_type=jnp.float32)
    grad_gain_one = jnp.sum(grad_hidden_one * normed_one, axis=0)
    grad_shift_one = jnp.sum(grad_hidden_one, axis=0)
    grad_input = grad_residual + norm_back(grad_hidden_one, normed_one, inverse_one, gain_one)
    attn_terms = (
        grad_weight_qkv,
        grad_weight_out,
        grad_gain_one,
        grad_shift_one,
        grad_bias_qv,
        grad_bias_out,
    )
    attn_summed = lax.psum(
        (attn_terms[0], attn_terms[1], attn_terms[2], attn_terms[3], attn_terms[4], attn_terms[5]),
        "seq",
    )
    attn_grads = (
        lax.psum_scatter(attn_summed[0], "dp", scatter_dimension=0, tiled=True),
        lax.psum_scatter(attn_summed[1], "dp", scatter_dimension=0, tiled=True),
        lax.psum_scatter(attn_summed[2], "dp", scatter_dimension=0, tiled=True),
        lax.psum_scatter(attn_summed[3], "dp", scatter_dimension=0, tiled=True),
        lax.psum_scatter(attn_summed[4], "dp", scatter_dimension=0, tiled=True),
        lax.psum_scatter(attn_summed[5], "dp", scatter_dimension=0, tiled=True),
    )
    return (
        frames_out,
        grad_input.reshape(shape_local),
        attn_grads[2],
        attn_grads[3],
        attn_grads[0],
        attn_grads[4],
        attn_grads[1],
        attn_grads[5],
        mlp_grads[2],
        mlp_grads[3],
        mlp_grads[0],
        mlp_grads[4],
        mlp_grads[1],
        mlp_grads[5],
    )


def solution(mesh):
    in_specs = (
        P("dp", "seq", None),
        P("dp"),
        P("dp"),
        P("dp", None),
        P("dp"),
        P("dp", None),
        P("dp"),
        P("dp"),
        P("dp"),
        P("dp", None),
        P("dp"),
        P("dp", None),
        P("dp"),
        P("dp", "seq", None),
    )
    out_specs = (
        P("dp", "seq", None),
        P("dp", "seq", None),
        P("dp"),
        P("dp"),
        P("dp", None),
        P("dp"),
        P("dp", None),
        P("dp"),
        P("dp"),
        P("dp"),
        P("dp", None),
        P("dp"),
        P("dp", None),
        P("dp"),
    )
    return jax.shard_map(shards, mesh=mesh, in_specs=in_specs, out_specs=out_specs, check_vma=False)
```

profile of v0, /device:TPU:0, one launch (start us, length us, event | category | flops | bytes accessed | tf_op | source)
XLA Modules:
  0.0 1038.6 jit_solution(15430332601258797024)
XLA Ops:
  19.4 64.0 %all-reduce.19 = (bf16[1536]{0:T(1024)(128)(2,1)S(1)}, bf16[768]{0:T(1024)(128)(2,1)S(1)}, bf16[768]{0:T(1024)(128)(2,1)S(1)}, bf16[768]{0:T(1024)(128)(2,1)S(1)...) all-reduce(bf16[1536]{0:T(1024)(128)(2,1)S(1)} %dynamic-update-slic, ...), channel_id=1, replica_groups=mesh['dp'=16,'seq'=2] {'dp'}, use_global_device_ids=true, to_apply=%add.2 | all-reduce | flops 9216 | bytes 36864
  99.0 9.1 reduce.13
  122.0 9.1 reduce.15
  146.3 9.1 reduce.14
  164.6 5.4 reshape.283
  213.2 42.6 %while.26 = (s32[]{:T(128)}, bf16[6,1500,64]{1,2,0:T(8,128)(2,1)}, f32[6,1500]{1,0:T(8,128)S(1)}, bf16[6,1500,64]{2,1,0:T(8,128)(2,1)S(1)}, bf16[6,1500,64]{2,1,...) while((s32[]{:T(128)}, bf16[6,1500,64]{1,2,0:T(8,128)(2,1)}, ...), condition=%wide.region_5.6_spmd, body=%wide.region_2.5_spmd.sunk | while | flops 589594496 | bytes 28419816 | solution.py:140
  255.8 6.6 copy.85
  262.4 10.9 %reduce.16 = bf16[1500,384]{1,0:T(8,128)(2,1)} reduce(bf16[1500,1,384]{2,1,0:T(2,128)(2,1)} %bitcast.268, bf16[]{:T(256)} %broadcast.144), dimensions={1}, to_apply=%bitcast.180.reduce_sub_computation | reduce | bytes 2304002
  281.6 10.9 %all-to-all-done.3 = bf16[2,2,144000]{2,1,0:T(2,128)(2,1)} async-done(((bf16[2,2,144000]{2,1,0:T(2,128)(2,1)}), bf16[2,2,144000]{2,1,0:T(2,128)(2,1)}, u32[]{:S(2)}, u32[]{:S(2)}) %all-to-all-start.3) | async-done | bytes 1152032 | tf_op jit(solution)/shard_map/all_to_all | solution.py:142
  292.5 5.7 reshape.289
  298.1 10.9 %bitcast_reduce_fusion.3 = bf16[1500,384]{1,0:T(8,128)(2,1)} fusion(bf16[1500,1,384]{2,1,0:T(2,128)(2,1)} %reshape.289), kind=kLoop, calls=%fused_computation.142 | loop fusion | bytes 2304000 | tf_op jit(solution)/shard_map/all_to_all | solution.py:142
  318.6 10.8 %multiply_convert_fusion = (bf16[750,3072]{1,0:T(8,128)(2,1)}, f32[750,3072]{1,0:T(8,128)}) fusion(f32[3072]{0:T(1024)S(1)} %convert_element_type.111, bf16[768,3072]{1,0:T(8,128)(2,1)} %all-gather.9.cloned.1.call-done, f32[750,768]{1,0:T(8,128)} %copy-done, f32[768]{0:T(1024)S(1)} %convert_element_type.109, f32[768]{0:T(1024)S(1)} %convert_element_type.108, ...), kind=kOutput, calls=%fused_computation.62 | convolution fusion | flops 3555648000 | bytes 20871024 | tf_op jit(solution)/shard_map/dot_general | solution.py:160
  329.5 10.2 fusion.96
  353.5 9.1 reduce.17
  393.2 93.8 %while.27 = (s32[]{:T(128)}, bf16[6,1500,64]{1,2,0:T(8,128)(2,1)}, bf16[6,1500,64]{1,2,0:T(8,128)(2,1)}, bf16[6,1500,64]{1,2,0:T(8,128)(2,1)}, bf16[6,1500,64]{2...) while((s32[]{:T(128)}, bf16[6,1500,64]{1,2,0:T(8,128)(2,1)}, ...), condition=%wide.region_12.13_spmd, body=%wide.region_10.12_spmd.sunk | while | flops 1454362368 | bytes 45485876 | solution.py:212
  487.0 6.8 copy.94
  493.8 10.0 reduce.20
  516.3 9.9 reduce.19
  538.7 8.8 reduce.18
  559.1 10.1 bitcast_reduce_fusion
  576.6 9.9 bitcast_reduce_fusion.1
  594.0 9.9 bitcast_reduce_fusion.2
  607.3 8.3 fusion.72
  617.3 8.9 fusion.68
  626.3 10.9 %fusion.79 = f32[3072,768]{1,0:T(8,128)} fusion(bf16[750,3072]{1,0:T(8,128)(2,1)} %get-tuple-element.303, bf16[1,750,768]{2,1,0:T(8,128)(2,1)} %param.31), kind=kOutput, calls=%fused_computation.114 | convolution fusion | flops 3538944000 | bytes 15197184 | tf_op jit(solution)/shard_map/dot_general | solution.py:173
  639.4 9.1 fusion.75
  650.3 60.8 %reduce-scatter.5.cloned.1.call-done = f32[48,2304]{1,0:T(8,128)} async-done(((f32[768,2304]{1,0:T(8,128)}), f32[48,2304]{1,0:T(8,128)}) %reduce-scatter.5.cloned.1.call-update) | async-done | bytes 442384 | tf_op jit(solution)/shard_map/reduce_scatter | solution.py:262
  711.1 115.0 %reduce-scatter.9.cloned.1.call-done = f32[48,3072]{1,0:T(8,128)} async-done(((f32[768,3072]{1,0:T(8,128)}), f32[48,3072]{1,0:T(8,128)}) %reduce-scatter.9.cloned.1.call-update) | async-done | bytes 589840 | tf_op jit(solution)/shard_map/reduce_scatter | solution.py:196
  826.2 115.0 %reduce-scatter.11.cloned.1.call-done = f32[192,768]{1,0:T(8,128)} async-done(((f32[3072,768]{1,0:T(8,128)}), f32[192,768]{1,0:T(8,128)}) %reduce-scatter.11.cloned.1.call-update) | async-done | bytes 589840 | tf_op jit(solution)/shard_map/reduce_scatter | solution.py:197
  941.3 7.9 fusion.63
  949.3 60.9 %all-reduce.16 = (f32[768]{0:T(1024)S(1)}, f32[768]{0:T(1024)}, f32[1536]{0:T(1024)S(1)}, f32[768]{0:T(1024)}, f32[768]{0:T(1024)}, /*index=5*/f32[768]{0:T(1024)}, f32[3072]{0:T(1024)S(1)}, f32[768]{0:T(1024)}) all-reduce(f32[768]{0:T(1024)S(1)} %get-tuple-element.222, ...), channel_id=2, replica_groups=mesh['dp'=16,'seq'=2] {'dp'}, use_global_device_ids=true, to_apply=%region_17.18.clone | all-reduce | flops 9216 | bytes 73728
  1020.1 5.5 all-reduce.17
  (310 shorter events, 380.2 us)
Async XLA Ops:
  7.2 77.7 %copy-start.4 = (bf16[1,750,768]{2,1,0:T(8,128)(2,1)S(1)}, bf16[1,750,768]{2,1,0:T(8,128)(2,1)}, u32[]{:S(2)}) copy-start(bf16[1,750,768]{2,1,0:T(8,128)(2,1)} %param.18) | copy-start | bytes 3456004
  7.2 78.3 %all-gather.5.cloned.1.call-start = ((), (), s32[]{:S(2)}) async-start(), calls=%async_computation.12 | async-start | bytes 3760128 | tf_op jit(solution)/shard_map/all_gather | solution.py:109
  7.9 306.0 %all-gather.7.cloned.1.call-start = ((), (), s32[]{:S(2)}) async-start(), calls=%async_computation.13 | async-start | bytes 1253376 | tf_op jit(solution)/shard_map/all_gather | solution.py:110
  8.7 309.9 %all-gather.9.cloned.1.call-start = ((), (), s32[]{:S(2)}) async-start(), calls=%async_computation.14 | async-start | bytes 5013504 | tf_op jit(solution)/shard_map/all_gather | solution.py:148
  83.4 7.2 copy-start.25
  112.7 22.6 %all-to-all-start = ((bf16[2,2,144000]{2,1,0:T(2,128)(2,1)}), bf16[2,2,144000]{2,1,0:T(2,128)(2,1)}, u32[]{:S(2)}, u32[]{:S(2)}) async-start(bf16[2,2,144000]{2,1,0:T(2,128)(2,1)} %reshape.282), calls=%async_computation | async-start | bytes 2304000 | tf_op jit(solution)/shard_map/all_to_all | solution.py:129
  135.2 24.3 %all-to-all-start.2 = ((bf16[2,2,144000]{2,1,0:T(2,128)(2,1)}), bf16[2,2,144000]{2,1,0:T(2,128)(2,1)}, u32[]{:S(2)}, u32[]{:S(2)}) async-start(bf16[2,2,144000]{2,1,0:T(2,128)(2,1)} %reshape.286), calls=%async_computation.2 | async-start | bytes 2304000 | tf_op jit(solution)/shard_map/all_to_all | solution.py:133
  159.6 35.1 %all-to-all-start.1 = ((bf16[2,2,144000]{2,1,0:T(2,128)(2,1)}), bf16[2,2,144000]{2,1,0:T(2,128)(2,1)}, u32[]{:S(2)}, u32[]{:S(2)}) async-start(bf16[2,2,144000]{2,1,0:T(2,128)(2,1)} %reshape.284), calls=%async_computation.1 | async-start | bytes 2304000 | tf_op jit(solution)/shard_map/all_to_all | solution.py:130
  164.0 165.4 %all-gather.11.cloned.1.call-start = ((), (), s32[]{:S(2)}) async-start(), calls=%async_computation.15 | async-start | bytes 5013504 | tf_op jit(solution)/shard_map/all_gather | solution.py:149
  277.1 15.4 %all-to-all-start.3 = ((bf16[2,2,144000]{2,1,0:T(2,128)(2,1)}), bf16[2,2,144000]{2,1,0:T(2,128)(2,1)}, u32[]{:S(2)}, u32[]{:S(2)}) async-start(bf16[2,2,144000]{2,1,0:T(2,128)(2,1)} %reshape.288), calls=%async_computation.3 | async-start | bytes 2304000 | tf_op jit(solution)/shard_map/all_to_all | solution.py:142
  318.6 10.9 %copy-start.14 = (bf16[1,750,768]{2,1,0:T(8,128)(2,1)S(1)}, bf16[1,750,768]{2,1,0:T(8,128)(2,1)}, u32[]{:S(2)}) copy-start(bf16[1,750,768]{2,1,0:T(8,128)(2,1)} %param.31) | copy-start | bytes 3456004
  329.5 10.2 copy-start.1
  329.5 10.2 copy-start.30
  367.2 13.5 %all-to-all-start.4 = ((bf16[2,2,144000]{2,1,0:T(2,128)(2,1)}), bf16[2,2,144000]{2,1,0:T(2,128)(2,1)S(1)}, u32[]{:S(2)}, u32[]{:S(2)}) async-start(bf16[2,2,144000]{2,1,0:T(2,128)(2,1)} %reshape.290), calls=%async_computation.4 | async-start | bytes 2304000 | tf_op jit(solution)/shard_map/all_to_all | solution.py:209
  370.8 279.5 %reduce-scatter.7.cloned.1.call-start = ((), (), s32[]{:S(2)}) async-start(), calls=%async_computation.17 | async-start | bytes 2506752 | tf_op jit(solution)/shard_map/reduce_scatter | solution.py:263
  503.8 8.3 copy-start.10
  507.7 22.4 %all-to-all-start.5 = ((bf16[2,2,144000]{2,1,0:T(2,128)(2,1)}), bf16[2,2,144000]{2,1,0:T(2,128)(2,1)}, u32[]{:S(2)}, u32[]{:S(2)}) async-start(bf16[2,2,144000]{2,1,0:T(2,128)(2,1)} %reshape.296), calls=%async_computation.5 | async-start | bytes 2304000 | tf_op jit(solution)/shard_map/all_to_all | solution.py:224
  526.1 8.4 copy-start.11
  530.0 24.5 %all-to-all-start.6 = ((bf16[2,2,144000]{2,1,0:T(2,128)(2,1)}), bf16[2,2,144000]{2,1,0:T(2,128)(2,1)}, u32[]{:S(2)}, u32[]{:S(2)}) async-start(bf16[2,2,144000]{2,1,0:T(2,128)(2,1)} %reshape.294), calls=%async_computation.6 | async-start | bytes 2304000 | tf_op jit(solution)/shard_map/all_to_all | solution.py:227
  554.6 34.9 %all-to-all-start.7 = ((bf16[2,2,144000]{2,1,0:T(2,128)(2,1)}), bf16[2,2,144000]{2,1,0:T(2,128)(2,1)}, u32[]{:S(2)}, u32[]{:S(2)}) async-start(bf16[2,2,144000]{2,1,0:T(2,128)(2,1)} %reshape.292), calls=%async_computation.7 | async-start | bytes 2304000 | tf_op jit(solution)/shard_map/all_to_all | solution.py:230
  559.1 152.1 %reduce-scatter.5.cloned.1.call-start = ((), (), s32[]{:S(2)}) async-start(), calls=%async_computation.16 | async-start | bytes 7520256 | tf_op jit(solution)/shard_map/reduce_scatter | solution.py:262
  605.4 10.2 copy-start.3
  615.7 210.5 %reduce-scatter.9.cloned.1.call-start = ((), (), s32[]{:S(2)}) async-start(), calls=%async_computation.18 | async-start | bytes 10027008 | tf_op jit(solution)/shard_map/reduce_scatter | solution.py:196
  626.2 315.0 %reduce-scatter.11.cloned.1.call-start = ((), (), s32[]{:S(2)}) async-start(), calls=%async_computation.19 | async-start | bytes 10027008 | tf_op jit(solution)/shard_map/reduce_scatter | solution.py:197
  637.2 388.5 %all-reduce.22.cloned.1.call-start = ((), (), s32[]{:S(2)}) async-start(), calls=%async_computation.20 | async-start | bytes 3538944 | tf_op jit(solution)/shard_map/psum | solution.py:257
  648.5 292.8 %copy-start.6 = (bf16[1,750,768]{2,1,0:T(8,128)(2,1)S(1)}, bf16[1,750,768]{2,1,0:T(8,128)(2,1)}, u32[]{:S(2)}) copy-start(bf16[1,750,768]{2,1,0:T(8,128)(2,1)} %param.18) | copy-start | bytes 3456004
  941.2 8.0 copy-start.18
  941.2 8.0 copy-start.19
  941.2 8.0 copy-start.24
  941.3 8.0 copy-start.27
  941.3 8.0 copy-start.28
  941.3 72.7 %copy-start.8 = (f32[750,768]{1,0:T(8,128)S(1)}, f32[750,768]{1,0:T(8,128)}, u32[]{:S(2)}) copy-start(f32[750,768]{1,0:T(8,128)} %copy-done.7) | copy-start | bytes 6912004
  (17 other events, 63.1 us)
Sparse Core Ops, SparseCore 0:
  10.3 50.1 all-gather.4
  62.8 36.8 all-gather.6
  101.9 51.9 all-gather.8
  166.8 50.9 all-gather.10
  375.5 62.9 reduce-scatter.6
  615.8 95.3 reduce-scatter.4
  715.2 110.9 reduce-scatter.8
  830.3 110.8 reduce-scatter.10
  943.7 55.5 all-reduce.21
where the time goes:
time: 1050 us; the launch traced here: 1040 us
  waiting for transfers between devices  310 us (30%)
  local copies, waits for them, and re-layouts  248 us (24%)
  matrix products  200 us (19%)
  blocking collectives  130 us (12%)
  other arithmetic  95.8 us (9%)
  starting transfers between devices  35.5 us (3%)
  between operations  18.6 us (2%)
    unnamed x2, blocking collectives  125 us
    reduce_scatter x1, waiting for transfers between devices, shards(): lax.psum_scatter(mlp_summed[0], 'dp', scatter_dimension=0, tiled=True)  115 us
    reduce_scatter x1, waiting for transfers between devices, shards(): lax.psum_scatter(mlp_summed[1], 'dp', scatter_dimension=0, tiled=True)  115 us
    unnamed x115, local copies, waits for them, and re-layouts  107 us
    unnamed x8, other arithmetic  76.1 us
    reduce_scatter x1, waiting for transfers between devices, shards(): lax.psum_scatter(attn_summed[0], 'dp', scatter_dimension=0, tiled=True)  60.8 us
    reshape x4, local copies, waits for them, and re-layouts, from_heads(): return joined.reshape(clip_count, frame_count, group_heads * head_size)  21.6 us
  transfers between devices with their start and end apart: 17, of which 5 were waited for; matrix products, arithmetic and copies ran while one was open for 47% of the time, Pallas kernels for 0%

commit v1 on v0

--- a/solution.py
+++ b/solution.py
@@ -1,3 +1,4 @@
+import functools
 import math
 import jax
 import jax.numpy as jnp
@@ -6,6 +7,22 @@
 
 HEADS = 12
 EPSILON = 1e-05
+
+
+def keep_up_leaf_here(packet, dev_axis):
+    val2 = jnp.concatenate(
+        lax.all_to_all(
+            jnp.stack(jnp.split(packet, lax.axis_size(dev_axis), axis=1)),
+            axis_name=dev_axis,
+            concat_axis=0,
+            split_axis=0,
+        ),
+        axis=2,
+    )
+    return val2
+
+
+check_digits = functools.partial(keep_up_leaf_here, dev_axis="seq")
 
 
 def normalize(values, gain, shift):
@@ -139,9 +156,7 @@
     value_heads = to_heads(value_group, head_size)
     context_heads, logsum = lax.map(head_forward, (query_heads, key_heads, value_heads))
     context_heads = lax.optimization_barrier(context_heads)
-    context = lax.all_to_all(
-        from_heads(context_heads, clip_count), "seq", split_axis=1, concat_axis=2, tiled=True
-    )
+    context = check_digits(from_heads(context_heads, clip_count))
     context = context.reshape(token_rows, features)
     residual = inputs + jnp.dot(context, out_full, preferred_element_type=jnp.float32) + bias_out
     mlp_full = (

time: 1050 us -> 1020 us (0.971)
  local copies, waits for them, and re-layouts: 248 us -> 222 us
    all_to_all x3 -> x0, local copies, waits for them, and re-layouts: 15.8 us -> none  [shards(): lax.all_to_all(from_heads(context_heads, clip_count), 'seq', split_axis=1...]
    unnamed x8 -> x7, other arithmetic: 76.1 us -> 65.5 us
    unnamed x115 -> x113, local copies, waits for them, and re-layouts: 107 us -> 96.6 us
    reshape x4 -> x3, local copies, waits for them, and re-layouts: 21.6 us -> 15.1 us  [from_heads(): return joined.reshape(clip_count, frame_count, group_heads * head_size)]
  transfers between devices with their start and end apart: 17 -> 17, of which waited for: 5 -> 5; matrix products, arithmetic and copies ran while one was open for 47% -> 45% of each run, Pallas kernels for 0% -> 0%
where the time goes in v1:
time: 1020 us; the launch traced here: 1000 us
  waiting for transfers between devices  310 us (30%)
  local copies, waits for them, and re-layouts  222 us (22%)
  matrix products  200 us (20%)
  blocking collectives  130 us (13%)
  other arithmetic  86.3 us (8%)
  starting transfers between devices  35.6 us (3%)
  between operations  18.8 us (2%)
    unnamed x2, blocking collectives  125 us
    reduce_scatter x1, waiting for transfers between devices, shards(): lax.psum_scatter(mlp_summed[0], 'dp', scatter_dimension=0, tiled=True)  115 us
    reduce_scatter x1, waiting for transfers between devices, shards(): lax.psum_scatter(mlp_summed[1], 'dp', scatter_dimension=0, tiled=True)  115 us
    unnamed x113, local copies, waits for them, and re-layouts  96.6 us
    unnamed x7, other arithmetic  65.5 us
    reduce_scatter x1, waiting for transfers between devices, shards(): lax.psum_scatter(attn_summed[0], 'dp', scatter_dimension=0, tiled=True)  60.9 us
    dot_general x6, matrix products, head_backward(): jnp.dot(grad_context, value_rows.T, preferred_element_type=jnp.float32)  20.6 us
  transfers between devices with their start and end apart: 17, of which 5 were waited for; matrix products, arithmetic and copies ran while one was open for 45% of the time, Pallas kernels for 0%

profile of v1, /device:TPU:0, one launch (start us, length us, event | category | flops | bytes accessed | tf_op | source)
XLA Modules:
  0.0 1003.5 jit_solution(13989843017462850084)
XLA Ops:
  19.4 64.0 %all-reduce.19 = (bf16[1536]{0:T(1024)(128)(2,1)S(1)}, bf16[768]{0:T(1024)(128)(2,1)S(1)}, bf16[768]{0:T(1024)(128)(2,1)S(1)}, bf16[768]{0:T(1024)(128)(2,1)S(1)...) all-reduce(bf16[1536]{0:T(1024)(128)(2,1)S(1)} %dynamic-update-slic, ...), channel_id=1, replica_groups=mesh['dp'=16,'seq'=2] {'dp'}, use_global_device_ids=true, to_apply=%add.2 | all-reduce | flops 9216 | bytes 36864
  85.5 5.1 fusion.88
  99.0 9.1 reduce.11
  121.7 9.1 reduce.13
  146.3 9.1 reduce.12
  164.6 5.4 reshape.281
  177.6 5.2 reshape.285
  194.5 5.2 reshape.283
  212.9 42.7 %while.26 = (s32[]{:T(128)}, bf16[6,1500,64]{1,2,0:T(8,128)(2,1)}, f32[6,1500]{1,0:T(8,128)S(1)}, bf16[6,1500,64]{2,1,0:T(8,128)(2,1)S(1)}, bf16[6,1500,64]{2,1,...) while((s32[]{:T(128)}, bf16[6,1500,64]{1,2,0:T(8,128)(2,1)}, ...), condition=%wide.region_5.6_spmd, body=%wide.region_2.5_spmd.sunk | while | flops 589594496 | bytes 28419816 | solution.py:157
  265.1 11.0 %all-to-all-done.3 = bf16[2,1,750,384]{3,2,1,0:T(8,128)(2,1)} async-done(((bf16[2,1,750,384]{3,2,1,0:T(8,128)(2,1)}), bf16[2,1,750,384]{3,2,1,0:T(8,128)(2,1)}, u32[]{:S(2)}, u32[]{:S(2)}) %all-to-all-start.3) | async-done | bytes 1152032 | tf_op jit(solution)/shard_map/all_to_all | solution.py:14
  283.6 10.8 %multiply_convert_fusion = (bf16[750,3072]{1,0:T(8,128)(2,1)}, f32[750,3072]{1,0:T(8,128)}) fusion(f32[3072]{0:T(1024)S(1)} %convert_element_type.111, bf16[768,3072]{1,0:T(8,128)(2,1)} %all-gather.9.cloned.1.call-done, f32[750,768]{1,0:T(8,128)} %copy-done, f32[768]{0:T(1024)S(1)} %convert_element_type.109, f32[768]{0:T(1024)S(1)} %convert_element_type.108, ...), kind=kOutput, calls=%fused_computation.62 | convolution fusion | flops 3555648000 | bytes 20871024 | tf_op jit(solution)/shard_map/dot_general | solution.py:175
  294.4 10.0 fusion.96
  318.4 9.1 reduce.14
  339.8 5.4 all-to-all-done.4
  357.8 93.8 %while.27 = (s32[]{:T(128)}, bf16[6,1500,64]{1,2,0:T(8,128)(2,1)}, bf16[6,1500,64]{1,2,0:T(8,128)(2,1)}, bf16[6,1500,64]{1,2,0:T(8,128)(2,1)}, bf16[6,1500,64]{2...) while((s32[]{:T(128)}, bf16[6,1500,64]{1,2,0:T(8,128)(2,1)}, ...), condition=%wide.region_12.13_spmd, body=%wide.region_10.12_spmd.sunk | while | flops 1454362368 | bytes 45485876 | solution.py:227
  451.6 6.8 copy.91
  458.4 10.3 %reduce.17 = bf16[1500,384]{1,0:T(8,128)(2,1)} reduce(bf16[1500,1,384]{2,1,0:T(2,128)(2,1)S(1)} %bitcast.267, bf16[]{:T(256)} %broadcast.143), dimensions={1}, to_apply=%bitcast.190.reduce_sub_computation | reduce | bytes 2304002
  481.2 9.9 reduce.16
  503.6 8.8 reduce.15
  524.0 10.0 bitcast_reduce_fusion
  541.5 9.9 bitcast_reduce_fusion.1
  558.8 9.9 bitcast_reduce_fusion.2
  572.0 8.3 fusion.72
  582.0 8.9 fusion.68
  590.9 10.8 %fusion.79 = f32[3072,768]{1,0:T(8,128)} fusion(bf16[750,3072]{1,0:T(8,128)(2,1)} %get-tuple-element.305, bf16[1,750,768]{2,1,0:T(8,128)(2,1)} %param.31), kind=kOutput, calls=%fused_computation.115 | convolution fusion | flops 3538944000 | bytes 15197184 | tf_op jit(solution)/shard_map/dot_general | solution.py:188
  604.1 9.1 fusion.75
  615.0 60.9 %reduce-scatter.5.cloned.1.call-done = f32[48,2304]{1,0:T(8,128)} async-done(((f32[768,2304]{1,0:T(8,128)}), f32[48,2304]{1,0:T(8,128)}) %reduce-scatter.5.cloned.1.call-update) | async-done | bytes 442384 | tf_op jit(solution)/shard_map/reduce_scatter | solution.py:277
  675.9 115.0 %reduce-scatter.9.cloned.1.call-done = f32[48,3072]{1,0:T(8,128)} async-done(((f32[768,3072]{1,0:T(8,128)}), f32[48,3072]{1,0:T(8,128)}) %reduce-scatter.9.cloned.1.call-update) | async-done | bytes 589840 | tf_op jit(solution)/shard_map/reduce_scatter | solution.py:211
  790.9 115.0 %reduce-scatter.11.cloned.1.call-done = f32[192,768]{1,0:T(8,128)} async-done(((f32[3072,768]{1,0:T(8,128)}), f32[192,768]{1,0:T(8,128)}) %reduce-scatter.11.cloned.1.call-update) | async-done | bytes 589840 | tf_op jit(solution)/shard_map/reduce_scatter | solution.py:212
  906.0 7.9 fusion.63
  914.0 60.9 %all-reduce.16 = (f32[768]{0:T(1024)S(1)}, f32[768]{0:T(1024)}, f32[1536]{0:T(1024)S(1)}, f32[768]{0:T(1024)}, f32[768]{0:T(1024)}, /*index=5*/f32[768]{0:T(1024)}, f32[3072]{0:T(1024)S(1)}, f32[768]{0:T(1024)}) all-reduce(f32[768]{0:T(1024)S(1)} %get-tuple-element.222, ...), channel_id=2, replica_groups=mesh['dp'=16,'seq'=2] {'dp'}, use_global_device_ids=true, to_apply=%region_17.18.clone | all-reduce | flops 9216 | bytes 73728
  984.9 5.5 all-reduce.17
  (307 shorter events, 358.0 us)
Async XLA Ops:
  7.2 77.7 %copy-start.4 = (bf16[1,750,768]{2,1,0:T(8,128)(2,1)S(1)}, bf16[1,750,768]{2,1,0:T(8,128)(2,1)}, u32[]{:S(2)}) copy-start(bf16[1,750,768]{2,1,0:T(8,128)(2,1)} %param.18) | copy-start | bytes 3456004
  7.2 78.3 %all-gather.5.cloned.1.call-start = ((), (), s32[]{:S(2)}) async-start(), calls=%async_computation.12 | async-start | bytes 3760128 | tf_op jit(solution)/shard_map/all_gather | solution.py:126
  7.9 270.9 %all-gather.7.cloned.1.call-start = ((), (), s32[]{:S(2)}) async-start(), calls=%async_computation.13 | async-start | bytes 1253376 | tf_op jit(solution)/shard_map/all_gather | solution.py:127
  8.7 274.9 %all-gather.9.cloned.1.call-start = ((), (), s32[]{:S(2)}) async-start(), calls=%async_computation.14 | async-start | bytes 5013504 | tf_op jit(solution)/shard_map/all_gather | solution.py:163
  83.4 7.2 copy-start.25
  112.4 22.6 %all-to-all-start = ((bf16[2,2,144000]{2,1,0:T(2,128)(2,1)}), bf16[2,2,144000]{2,1,0:T(2,128)(2,1)}, u32[]{:S(2)}, u32[]{:S(2)}) async-start(bf16[2,2,144000]{2,1,0:T(2,128)(2,1)} %reshape.280), calls=%async_computation | async-start | bytes 2304000 | tf_op jit(solution)/shard_map/all_to_all | solution.py:146
  135.0 24.5 %all-to-all-start.2 = ((bf16[2,2,144000]{2,1,0:T(2,128)(2,1)}), bf16[2,2,144000]{2,1,0:T(2,128)(2,1)}, u32[]{:S(2)}, u32[]{:S(2)}) async-start(bf16[2,2,144000]{2,1,0:T(2,128)(2,1)} %reshape.284), calls=%async_computation.2 | async-start | bytes 2304000 | tf_op jit(solution)/shard_map/all_to_all | solution.py:150
  159.5 35.0 %all-to-all-start.1 = ((bf16[2,2,144000]{2,1,0:T(2,128)(2,1)}), bf16[2,2,144000]{2,1,0:T(2,128)(2,1)}, u32[]{:S(2)}, u32[]{:S(2)}) async-start(bf16[2,2,144000]{2,1,0:T(2,128)(2,1)} %reshape.282), calls=%async_computation.1 | async-start | bytes 2304000 | tf_op jit(solution)/shard_map/all_to_all | solution.py:147
  164.0 130.4 %all-gather.11.cloned.1.call-start = ((), (), s32[]{:S(2)}) async-start(), calls=%async_computation.15 | async-start | bytes 5013504 | tf_op jit(solution)/shard_map/all_gather | solution.py:164
  260.6 15.5 %all-to-all-start.3 = ((bf16[2,1,750,384]{3,2,1,0:T(8,128)(2,1)}), bf16[2,1,750,384]{3,2,1,0:T(8,128)(2,1)}, u32[]{:S(2)}, u32[]{:S(2)}) async-start(bf16[2,1,750,384]{3,2,1,0:T(8,128)(2,1)} %copy.82), calls=%async_computation.3 | async-start | bytes 2310144 | tf_op jit(solution)/shard_map/all_to_all | solution.py:14
  283.5 10.9 %copy-start.14 = (bf16[1,750,768]{2,1,0:T(8,128)(2,1)S(1)}, bf16[1,750,768]{2,1,0:T(8,128)(2,1)}, u32[]{:S(2)}) copy-start(bf16[1,750,768]{2,1,0:T(8,128)(2,1)} %param.31) | copy-start | bytes 3456004
  294.4 10.0 copy-start.1
  294.4 10.0 copy-start.30
  331.6 13.5 %all-to-all-start.4 = ((bf16[2,2,144000]{2,1,0:T(2,128)(2,1)}), bf16[2,2,144000]{2,1,0:T(2,128)(2,1)S(1)}, u32[]{:S(2)}, u32[]{:S(2)}) async-start(bf16[2,2,144000]{2,1,0:T(2,128)(2,1)} %reshape.286), calls=%async_computation.4 | async-start | bytes 2304000 | tf_op jit(solution)/shard_map/all_to_all | solution.py:224
  335.2 279.8 %reduce-scatter.7.cloned.1.call-start = ((), (), s32[]{:S(2)}) async-start(), calls=%async_computation.17 | async-start | bytes 2506752 | tf_op jit(solution)/shard_map/reduce_scatter | solution.py:278
  468.7 8.4 copy-start.10
  472.6 22.4 %all-to-all-start.5 = ((bf16[2,2,144000]{2,1,0:T(2,128)(2,1)}), bf16[2,2,144000]{2,1,0:T(2,128)(2,1)}, u32[]{:S(2)}, u32[]{:S(2)}) async-start(bf16[2,2,144000]{2,1,0:T(2,128)(2,1)} %reshape.292), calls=%async_computation.5 | async-start | bytes 2304000 | tf_op jit(solution)/shard_map/all_to_all | solution.py:239
  491.1 8.3 copy-start.11
  495.0 24.5 %all-to-all-start.6 = ((bf16[2,2,144000]{2,1,0:T(2,128)(2,1)}), bf16[2,2,144000]{2,1,0:T(2,128)(2,1)}, u32[]{:S(2)}, u32[]{:S(2)}) async-start(bf16[2,2,144000]{2,1,0:T(2,128)(2,1)} %reshape.290), calls=%async_computation.6 | async-start | bytes 2304000 | tf_op jit(solution)/shard_map/all_to_all | solution.py:242
  519.5 34.9 %all-to-all-start.7 = ((bf16[2,2,144000]{2,1,0:T(2,128)(2,1)}), bf16[2,2,144000]{2,1,0:T(2,128)(2,1)}, u32[]{:S(2)}, u32[]{:S(2)}) async-start(bf16[2,2,144000]{2,1,0:T(2,128)(2,1)} %reshape.288), calls=%async_computation.7 | async-start | bytes 2304000 | tf_op jit(solution)/shard_map/all_to_all | solution.py:245
  524.0 151.9 %reduce-scatter.5.cloned.1.call-start = ((), (), s32[]{:S(2)}) async-start(), calls=%async_computation.16 | async-start | bytes 7520256 | tf_op jit(solution)/shard_map/reduce_scatter | solution.py:277
  570.3 10.0 copy-start.3
  580.3 210.6 %reduce-scatter.9.cloned.1.call-start = ((), (), s32[]{:S(2)}) async-start(), calls=%async_computation.18 | async-start | bytes 10027008 | tf_op jit(solution)/shard_map/reduce_scatter | solution.py:211
  590.9 315.0 %reduce-scatter.11.cloned.1.call-start = ((), (), s32[]{:S(2)}) async-start(), calls=%async_computation.19 | async-start | bytes 10027008 | tf_op jit(solution)/shard_map/reduce_scatter | solution.py:212
  601.8 388.6 %all-reduce.22.cloned.1.call-start = ((), (), s32[]{:S(2)}) async-start(), calls=%async_computation.20 | async-start | bytes 3538944 | tf_op jit(solution)/shard_map/psum | solution.py:272
  613.2 292.8 %copy-start.6 = (bf16[1,750,768]{2,1,0:T(8,128)(2,1)S(1)}, bf16[1,750,768]{2,1,0:T(8,128)(2,1)}, u32[]{:S(2)}) copy-start(bf16[1,750,768]{2,1,0:T(8,128)(2,1)} %param.18) | copy-start | bytes 3456004
  906.0 8.0 copy-start.18
  906.0 8.0 copy-start.19
  906.0 8.0 copy-start.24
  906.0 8.0 copy-start.27
  906.0 8.0 copy-start.28
  906.0 72.7 %copy-start.8 = (f32[750,768]{1,0:T(8,128)S(1)}, f32[750,768]{1,0:T(8,128)}, u32[]{:S(2)}) copy-start(f32[750,768]{1,0:T(8,128)} %copy-done.7) | copy-start | bytes 6912004
  (17 other events, 62.2 us)
Sparse Core Ops, SparseCore 0:
  10.3 50.1 all-gather.4
  62.8 36.8 all-gather.6
  101.9 51.9 all-gather.8
  166.8 50.9 all-gather.10
  339.9 63.1 reduce-scatter.6
  580.5 95.3 reduce-scatter.4
  680.0 110.9 reduce-scatter.8
  795.0 110.8 reduce-scatter.10
  908.4 55.5 all-reduce.21
